TPU v7x, 128 devices: a whole 4x4x4 slice. The times are simulated.
128 devices in a mesh: row: 16 (over z_hi, y, core), col: 8 (over z_lo, x).
Axes of the slice: x: 4, y: 4, z: 4 (z_hi: 2, z_lo: 2; z = z_hi * 2 + z_lo), core: 2. Of those that a mesh axis runs over, the one named last changes fastest.
Arguments:
- grad_out: bfloat16 [262144, 256], P(('row', 'col')), may hold values from -6 to 6
- preact: bfloat16 [262144, 256], P(('row', 'col')), may hold values from -6 to 6
- features: bfloat16 [262144, 256], P(('col', 'row')), may hold values from -6 to 6
- weight: bfloat16 [256, 256], replicated, may hold values from -0.375 to 0.375
- tiles: bfloat16 [16, 8, 320, 128, 128], P('row', 'col'), may hold values from -0.099609375 to 0.099609375
- tile_rows: int32 [16, 8, 320], P('row', 'col'), may hold values from 0 to 127
- tile_cols: int32 [16, 8, 320], P('row', 'col'), may hold values from 0 to 255
- live_counts: int32 [16, 8], P('row', 'col'), may hold values from 80 to 320, as said below
Outputs:
- grad_features: bfloat16 [262144, 256], P(('col', 'row'))
- grad_weight: float32 [256, 256], replicated
Inputs may be any that keep to these rules, and one draw needn't show every extreme that they name: `live_counts`: some block holds exactly 320 live tiles in every draw.
All inputs are finite; a program needn't handle non-finite values.
Results may differ from a plain program's by a relative error of at most 0.02.
Values may be sent and summed in bfloat16 or wider, within the bound.
A program may use at most 192 MiB of HBM per device.

v0:
```python
import math
import jax
import jax.numpy as jnp
from jax import lax
from jax.sharding import PartitionSpec as P


def body(grad_out, preact, features, weight, tiles, tile_rows, tile_cols, live_counts):
    width = grad_out.shape[1]
    masked = jnp.where(preact > 0, grad_out, jnp.zeros_like(grad_out))
    block = lax.all_gather(masked, "col", axis=0, tiled=True)
    row_count = block.shape[0] // 128
    row_flat = block.reshape(row_count, 128 * width)
    slots = tiles.shape[2]
    tile_stack = tiles.reshape(slots, 128, 128)
    row_index = tile_rows.reshape(slots)
    col_index = tile_cols.reshape(slots)
    count = live_counts.reshape(())
    col_tiles = lax.axis_size("row") * grad_out.shape[0] // 128
    group = math.gcd(slots, 32)
    offsets = jnp.arange(group, dtype=jnp.int32)
    row_ids = jnp.arange(row_count, dtype=jnp.int32)
    col_ids = jnp.arange(col_tiles, dtype=jnp.int32)

    def add_group(step, accum):
        start = step * group
        tile_blk = lax.dynamic_slice_in_dim(tile_stack, start, group, 0)
        rows_now = lax.dynamic_slice_in_dim(row_index, start, group, 0)
        cols_now = lax.dynamic_slice_in_dim(col_index, start, group, 0) - 0
        pick = (rows_now[:, None] == row_ids[None, :]).astype(jnp.bfloat16)
        gathered = jnp.dot(pick, row_flat, preferred_element_type=jnp.float32).astype(jnp.bfloat16)
        gathered = gathered.reshape(group, 128, width)
        prod = jnp.einsum("kab,kaf->kbf", tile_blk, gathered, preferred_element_type=jnp.float32)
        upper = prod.astype(jnp.bfloat16)
        lower = (prod - upper.astype(jnp.float32)).astype(jnp.bfloat16)
        keep = start + offsets < count
        place = ((cols_now[None, :] == col_ids[:, None]) & keep[None, :]).astype(jnp.bfloat16)
        both_place = jnp.concatenate([place, place], axis=1)
        both_vals = jnp.concatenate([upper, lower], axis=0).reshape(2 * group, 128 * width)
        return accum + jnp.dot(both_place, both_vals, preferred_element_type=jnp.float32)

    accum = jnp.zeros((col_tiles, 128 * width), jnp.float32)
    accum = lax.fori_loop(0, slots // group, add_group, accum)
    partial_value = accum.reshape(col_tiles * 128, width)
    summed = lax.psum_scatter(
        partial_value.astype(jnp.bfloat16), "row", scatter_dimension=0, tiled=True
    )
    grad_features = lax.dot_general(
        summed, weight, (((1,), (1,)), ((), ())), preferred_element_type=jnp.float32
    ).astype(jnp.bfloat16)
    weight_term = lax.dot_general(
        features, summed, (((0,), (0,)), ((), ())), preferred_element_type=jnp.float32
    )
    grad_weight = lax.psum(weight_term, ("row", "col"))
    return (grad_features, grad_weight)


def solution(mesh):
    in_specs = (
        P(("row", "col"), None),
        P(("row", "col"), None),
        P(("col", "row"), None),
        P(),
        P("row", "col", None, None, None),
        P("row", "col", None),
        P("row", "col", None),
        P("row", "col"),
    )
    out_specs = (P(("col", "row"), None), P())
    return jax.shard_map(body, mesh=mesh, in_specs=in_specs, out_specs=out_specs, check_vma=False)
```

profile of v0, /device:TPU:1, one launch (start us, length us, event | category | flops | bytes accessed | tf_op | source)
XLA Modules:
  0.0 803.8 jit_solution(6973166508205975980)
XLA Ops:
  7.2 2.7 compare_select_fusion
  10.1 14.5 %copy.12 = bf16[1,1,320,128,128]{3,4,2,1,0:T(8,128)(2,1)} copy(bf16[1,1,320,128,128]{4,3,2,1,0:T(8,128)(2,1)} %param.14) | data formatting | bytes 20971520 | tf_op args[4]
  24.6 80.9 %all-gather.2.cloned.1.call-done = bf16[16384,256]{1,0:T(8,128)(2,1)} async-done(((bf16[2048,256]{1,0:T(8,128)(2,1)}), bf16[16384,256]{1,0:T(8,128)(2,1)}) %all-gather.2.cloned.1.call-update) | async-done | bytes 8388624 | tf_op jit(solution)/shard_map/all_gather | solution.py:11
  105.4 13.4 %reshape.49 = bf16[128,32768]{1,0:T(8,128)(2,1)} reshape(bf16[16384,256]{1,0:T(8,128)(2,1)} %all-gather.2.cloned.1.call-done) | data formatting | bytes 16777216 | tf_op jit(solution)/shard_map/reshape | solution.py:13
  118.9 342.9 %while.14 = (s32[]{:T(128)}, f32[256,32768]{1,0:T(8,128)}, s32[320]{0:T(512)S(1)}, s32[]{:T(128)}, bf16[320,128,128]{1,2,0:T(8,128)(2,1)}, /*index=5*/s32[320]{0...) while((s32[]{:T(128)}, f32[256,32768]{1,0:T(8,128)}, ...), condition=%wide.region_1.2_spmd.clone, body=%wide.region_0.1_spmd.clone.sunk | while | flops 1634766848 | bytes 110117888 | solution.py:43
  119.8 4.6 convolution_convert_fusion.3
  124.9 1.9 subtract_convert_fusion.2
  127.3 2.6 copy.19
  129.8 12.4 %convolution_add_fusion.2 = f32[256,32768]{1,0:T(8,128)} fusion(bf16[64,32768]{1,0:T(8,128)(2,1)S(1)} %bitcast.29, f32[256,32768]{1,0:T(8,128)} %get-tuple-element.281, pred[]{:T(512)S(6)} %compare.3, pred[256,32]{0,1:T(32,128)(4,1)S(1)} %fusion.34), kind=kOutput, calls=%fused_computation.3.clone.1 | convolution fusion | flops 1090535424 | bytes 71311360 | tf_op jit(solution)/shard_map/while/body/eval_jaxpr/dot_general | solution.py:40
  143.2 4.6 convolution_convert_fusion.3
  148.3 1.9 subtract_convert_fusion.2
  150.6 2.6 copy.19
  153.2 24.6 %convolution_add_fusion.2 = f32[256,32768]{1,0:T(8,128)} fusion(bf16[64,32768]{1,0:T(8,128)(2,1)S(1)} %bitcast.29, f32[256,32768]{1,0:T(8,128)} %get-tuple-element.281, pred[]{:T(512)S(6)} %compare.3, pred[256,32]{0,1:T(32,128)(4,1)S(1)} %fusion.34), kind=kOutput, calls=%fused_computation.3.clone.1 | convolution fusion | flops 1090535424 | bytes 71311360 | tf_op jit(solution)/shard_map/while/body/eval_jaxpr/dot_general | solution.py:40
  178.7 4.6 convolution_convert_fusion.3
  183.8 1.9 subtract_convert_fusion.2
  186.1 2.6 copy.19
  188.7 24.6 %convolution_add_fusion.2 = f32[256,32768]{1,0:T(8,128)} fusion(bf16[64,32768]{1,0:T(8,128)(2,1)S(1)} %bitcast.29, f32[256,32768]{1,0:T(8,128)} %get-tuple-element.281, pred[]{:T(512)S(6)} %compare.3, pred[256,32]{0,1:T(32,128)(4,1)S(1)} %fusion.34), kind=kOutput, calls=%fused_computation.3.clone.1 | convolution fusion | flops 1090535424 | bytes 71311360 | tf_op jit(solution)/shard_map/while/body/eval_jaxpr/dot_general | solution.py:40
  214.2 4.6 convolution_convert_fusion.3
  219.3 1.9 subtract_convert_fusion.2
  221.6 2.6 copy.19
  224.2 24.6 %convolution_add_fusion.2 = f32[256,32768]{1,0:T(8,128)} fusion(bf16[64,32768]{1,0:T(8,128)(2,1)S(1)} %bitcast.29, f32[256,32768]{1,0:T(8,128)} %get-tuple-element.281, pred[]{:T(512)S(6)} %compare.3, pred[256,32]{0,1:T(32,128)(4,1)S(1)} %fusion.34), kind=kOutput, calls=%fused_computation.3.clone.1 | convolution fusion | flops 1090535424 | bytes 71311360 | tf_op jit(solution)/shard_map/while/body/eval_jaxpr/dot_general | solution.py:40
  249.7 4.6 convolution_convert_fusion.3
  254.8 1.9 subtract_convert_fusion.2
  257.1 2.6 copy.19
  259.7 24.6 %convolution_add_fusion.2 = f32[256,32768]{1,0:T(8,128)} fusion(bf16[64,32768]{1,0:T(8,128)(2,1)S(1)} %bitcast.29, f32[256,32768]{1,0:T(8,128)} %get-tuple-element.281, pred[]{:T(512)S(6)} %compare.3, pred[256,32]{0,1:T(32,128)(4,1)S(1)} %fusion.34), kind=kOutput, calls=%fused_computation.3.clone.1 | convolution fusion | flops 1090535424 | bytes 71311360 | tf_op jit(solution)/shard_map/while/body/eval_jaxpr/dot_general | solution.py:40
  285.2 4.6 convolution_convert_fusion.3
  290.3 1.9 subtract_convert_fusion.2
  292.6 2.6 copy.19
  295.2 24.6 %convolution_add_fusion.2 = f32[256,32768]{1,0:T(8,128)} fusion(bf16[64,32768]{1,0:T(8,128)(2,1)S(1)} %bitcast.29, f32[256,32768]{1,0:T(8,128)} %get-tuple-element.281, pred[]{:T(512)S(6)} %compare.3, pred[256,32]{0,1:T(32,128)(4,1)S(1)} %fusion.34), kind=kOutput, calls=%fused_computation.3.clone.1 | convolution fusion | flops 1090535424 | bytes 71311360 | tf_op jit(solution)/shard_map/while/body/eval_jaxpr/dot_general | solution.py:40
  320.7 4.6 convolution_convert_fusion.3
  325.8 1.9 subtract_convert_fusion.2
  328.1 2.6 copy.19
  330.7 24.6 %convolution_add_fusion.2 = f32[256,32768]{1,0:T(8,128)} fusion(bf16[64,32768]{1,0:T(8,128)(2,1)S(1)} %bitcast.29, f32[256,32768]{1,0:T(8,128)} %get-tuple-element.281, pred[]{:T(512)S(6)} %compare.3, pred[256,32]{0,1:T(32,128)(4,1)S(1)} %fusion.34), kind=kOutput, calls=%fused_computation.3.clone.1 | convolution fusion | flops 1090535424 | bytes 71311360 | tf_op jit(solution)/shard_map/while/body/eval_jaxpr/dot_general | solution.py:40
  356.2 4.6 convolution_convert_fusion.3
  363.6 2.6 copy.19
  366.2 24.6 %convolution_add_fusion.2 = f32[256,32768]{1,0:T(8,128)} fusion(bf16[64,32768]{1,0:T(8,128)(2,1)S(1)} %bitcast.29, f32[256,32768]{1,0:T(8,128)} %get-tuple-element.281, pred[]{:T(512)S(6)} %compare.3, pred[256,32]{0,1:T(32,128)(4,1)S(1)} %fusion.34), kind=kOutput, calls=%fused_computation.3.clone.1 | convolution fusion | flops 1090535424 | bytes 71311360 | tf_op jit(solution)/shard_map/while/body/eval_jaxpr/dot_general | solution.py:40
  391.7 4.6 convolution_convert_fusion.3
  399.2 2.6 copy.19
  401.7 24.6 %convolution_add_fusion.2 = f32[256,32768]{1,0:T(8,128)} fusion(bf16[64,32768]{1,0:T(8,128)(2,1)S(1)} %bitcast.29, f32[256,32768]{1,0:T(8,128)} %get-tuple-element.281, pred[]{:T(512)S(6)} %compare.3, pred[256,32]{0,1:T(32,128)(4,1)S(1)} %fusion.34), kind=kOutput, calls=%fused_computation.3.clone.1 | convolution fusion | flops 1090535424 | bytes 71311360 | tf_op jit(solution)/shard_map/while/body/eval_jaxpr/dot_general | solution.py:40
  427.2 4.6 convolution_convert_fusion.3
  434.7 2.6 copy.19
  437.2 24.6 %convolution_add_fusion.2 = f32[256,32768]{1,0:T(8,128)} fusion(bf16[64,32768]{1,0:T(8,128)(2,1)S(1)} %bitcast.29, f32[256,32768]{1,0:T(8,128)} %get-tuple-element.281, pred[]{:T(512)S(6)} %compare.3, pred[256,32]{0,1:T(32,128)(4,1)S(1)} %fusion.34), kind=kOutput, calls=%fused_computation.3.clone.1 | convolution fusion | flops 1090535424 | bytes 71311360 | tf_op jit(solution)/shard_map/while/body/eval_jaxpr/dot_general | solution.py:40
  461.8 17.1 %convert_element_type.45 = bf16[256,32768]{1,0:T(8,128)(2,1)} convert(f32[256,32768]{1,0:T(8,128)} %get-tuple-element.171) | non-fusion elementwise | flops 8388608 | bytes 50331648 | tf_op jit(solution)/shard_map/convert_element_type | solution.py:46
  478.9 25.6 %convert_element_type.46 = bf16[32768,256]{1,0:T(8,128)(2,1)} reshape(bf16[256,32768]{1,0:T(8,128)(2,1)} %convert_element_type.45) | data formatting | bytes 33554432 | tf_op jit(solution)/shard_map/convert_element_type | solution.py:46
  504.6 145.1 %reduce-scatter.2.cloned.1.call-done = bf16[2048,256]{1,0:T(8,128)(2,1)} async-done(((bf16[32768,256]{1,0:T(8,128)(2,1)}), bf16[2048,256]{1,0:T(8,128)(2,1)}) %reduce-scatter.2.cloned.1.call-update) | async-done | bytes 1048592 | tf_op jit(solution)/shard_map/reduce_scatter | solution.py:45
  649.7 2.4 convolution_bitcast_fusion
  652.1 2.7 convolution_convert_fusion.1
  654.8 140.8 %all-reduce.2.cloned.1.call-done = f32[256,256]{0,1:T(8,128)} async-done(((f32[256,256]{0,1:T(8,128)}), f32[256,256]{0,1:T(8,128)}) %all-reduce.2.cloned.1.call-update) | async-done | bytes 262160 | tf_op jit(solution)/shard_map/psum | solution.py:54
  (81 shorter events, 25.2 us)
Async XLA Ops:
  7.2 642.5 %copy-start = (bf16[2048,256]{1,0:T(8,128)(2,1)S(1)}, bf16[2048,256]{1,0:T(8,128)(2,1)}, u32[]{:S(2)}) copy-start(bf16[2048,256]{1,0:T(8,128)(2,1)} %param.12) | copy-start | bytes 3145732
  7.2 2.9 copy-start.2
  7.2 2.9 copy-start.3
  7.2 98.2 %all-gather.2.cloned.1.call-start = ((), (), s32[]{:S(2)}) async-start(), calls=%async_computation.1 | async-start | bytes 9437184 | tf_op jit(solution)/shard_map/all_gather | solution.py:11
  10.0 639.7 %reduce-scatter.2.cloned.1.call-start = ((), (), s32[]{:S(2)}) async-start(), calls=%async_computation.2 | async-start | bytes 17825792 | tf_op jit(solution)/shard_map/reduce_scatter | solution.py:45
  504.5 147.6 %copy-start.1 = (bf16[256,256]{1,0:T(8,128)(2,1)S(1)}, bf16[256,256]{1,0:T(8,128)(2,1)}, u32[]{:S(2)}) copy-start(bf16[256,256]{1,0:T(8,128)(2,1)} %param.13) | copy-start | bytes 393220
  504.6 291.0 %all-reduce.2.cloned.1.call-start = ((), (), s32[]{:S(2)}) async-start(), calls=%async_computation.3 | async-start | bytes 524288 | tf_op jit(solution)/shard_map/psum | solution.py:54
Sparse Core Ops, SparseCore 0:
  10.3 95.1 all-gather.1
  504.7 144.9 reduce-scatter.1
  655.7 139.7 all-reduce.1
where the time goes:
time: 806 us; the launch traced here: 804 us
  waiting for transfers between devices  367 us (46%)
  matrix products  304 us (38%)
  local copies, waits for them, and re-layouts  87.5 us (11%)
  other arithmetic  30.8 us (4%)
  between operations  13.8 us (2%)
    dot_general x10, matrix products, add_group(): jnp.dot(both_place, both_vals, preferred_element_type=jnp.float32)  234 us
    reduce_scatter x1, waiting for transfers between devices, body(): lax.psum_scatter(partial_value.astype(jnp.bfloat16), 'row', scatter_dimen...  145 us
    psum x1, waiting for transfers between devices, body(): grad_weight = lax.psum(weight_term, ('row', 'col'))  141 us
    all_gather x1, waiting for transfers between devices, body(): block = lax.all_gather(masked, 'col', axis=0, tiled=True)  80.9 us
    dot_general x10, matrix products, add_group(): jnp.dot(pick, row_flat, preferred_element_type=jnp.float32)  46.4 us
    while x20, local copies, waits for them, and re-layouts  30.6 us
    convert_element_type x1, local copies, waits for them, and re-layouts, body(): partial_value.astype(jnp.bfloat16)  25.6 us
    dot_general x10, matrix products, add_group(): jnp.einsum('kab,kaf->kbf', tile_blk, gathered, preferred_element_type=jnp...  19.4 us
  transfers between devices with their start and end apart: 3, of which 3 were waited for; matrix products, arithmetic and copies ran while one was open for 2% of the time, Pallas kernels for 0%

commit v1 on v0

--- a/solution.py
+++ b/solution.py
@@ -3,6 +3,7 @@
 import jax.numpy as jnp
 from jax import lax
 from jax.sharding import PartitionSpec as P
+from jax.lax import all_gather
 
 
 def body(grad_out, preact, features, weight, tiles, tile_rows, tile_cols, live_counts):
@@ -51,7 +52,8 @@
     weight_term = lax.dot_general(
         features, summed, (((0,), (0,)), ((), ())), preferred_element_type=jnp.float32
     )
-    grad_weight = lax.psum(weight_term, ("row", "col"))
+    convert_slices_here = lambda arr, axis_name: jnp.sum(all_gather(arr, axis_name), axis=0)
+    grad_weight = convert_slices_here(weight_term, ("row", "col"))
     return (grad_features, grad_weight)
 
 

time: 806 us -> 1030 us (1.28)
  waiting for transfers between devices: 367 us -> 570 us
  local copies, waits for them, and re-layouts: 87.5 us -> 106 us
    all_gather x0 -> x1, waiting for transfers between devices: none -> 345 us  [body(): all_gather(arr, axis_name)]
    psum x1 -> x0, waiting for transfers between devices: 141 us -> none  [body(): grad_weight = lax.psum(weight_term, ('row', 'col'))]
    unnamed x10 -> x7, local copies, waits for them, and re-layouts: 16.3 us -> 34.9 us
where the time goes in v1:
time: 1030 us
  waiting for transfers between devices  570 us (55%)
  matrix products  304 us (30%)
  local copies, waits for them, and re-layouts  106 us (10%)
  other arithmetic  36.3 us (4%)
  between operations  13.8 us (1%)
    all_gather x1, waiting for transfers between devices, body(): all_gather(arr, axis_name)  345 us
    dot_general x10, matrix products, add_group(): jnp.dot(both_place, both_vals, preferred_element_type=jnp.float32)  234 us
    reduce_scatter x1, waiting for transfers between devices, body(): lax.psum_scatter(partial_value.astype(jnp.bfloat16), 'row', scatter_dimen...  145 us
    all_gather x1, waiting for transfers between devices, body(): block = lax.all_gather(masked, 'col', axis=0, tiled=True)  79.6 us
    dot_general x10, matrix products, add_group(): jnp.dot(pick, row_flat, preferred_element_type=jnp.float32)  46.4 us
    unnamed x7, local copies, waits for them, and re-layouts  34.9 us
    while x20, local copies, waits for them, and re-layouts  30.6 us
    convert_element_type x1, local copies, waits for them, and re-layouts, body(): partial_value.astype(jnp.bfloat16)  25.6 us
  transfers between devices with their start and end apart: 3, of which 3 were waited for; matrix products, arithmetic and copies ran while one was open for 2% of the time, Pallas kernels for 0%

profile of v1, /device:TPU:1, one launch (start us, length us, event | category | flops | bytes accessed | tf_op | source)
XLA Modules:
  0.0 1030.8 jit_solution(17158811552285771586)
XLA Ops:
  7.2 2.7 compare_select_fusion
  11.4 14.4 %copy.13 = bf16[1,1,320,128,128]{3,4,2,1,0:T(8,128)(2,1)} copy(bf16[1,1,320,128,128]{4,3,2,1,0:T(8,128)(2,1)} %param.14) | data formatting | bytes 20971520 | tf_op args[4]
  25.8 79.6 %all-gather.4.cloned.1.call-done = bf16[16384,256]{1,0:T(8,128)(2,1)} async-done(((bf16[2048,256]{1,0:T(8,128)(2,1)}), bf16[16384,256]{1,0:T(8,128)(2,1)}) %all-gather.4.cloned.1.call-update) | async-done | bytes 8388624 | tf_op jit(solution)/shard_map/all_gather | solution.py:12
  105.4 13.4 %reshape.49 = bf16[128,32768]{1,0:T(8,128)(2,1)} reshape(bf16[16384,256]{1,0:T(8,128)(2,1)} %all-gather.4.cloned.1.call-done) | data formatting | bytes 16777216 | tf_op jit(solution)/shard_map/reshape | solution.py:14
  118.9 342.9 %while.14 = (s32[]{:T(128)}, f32[256,32768]{1,0:T(8,128)}, s32[320]{0:T(512)S(1)}, s32[]{:T(128)}, bf16[320,128,128]{1,2,0:T(8,128)(2,1)}, /*index=5*/s32[320]{0...) while((s32[]{:T(128)}, f32[256,32768]{1,0:T(8,128)}, ...), condition=%wide.region_1.2_spmd.clone, body=%wide.region_0.1_spmd.clone.sunk | while | flops 1634766848 | bytes 110117888 | solution.py:44
  119.8 4.6 convolution_convert_fusion.3
  124.9 1.9 subtract_convert_fusion.2
  127.2 2.6 copy.21
  129.8 12.4 %convolution_add_fusion.2 = f32[256,32768]{1,0:T(8,128)} fusion(bf16[64,32768]{1,0:T(8,128)(2,1)S(1)} %bitcast.34, f32[256,32768]{1,0:T(8,128)} %get-tuple-element.281, pred[]{:T(512)S(6)} %compare.3, pred[256,32]{0,1:T(32,128)(4,1)S(1)} %fusion.34), kind=kOutput, calls=%fused_computation.3.clone.1 | convolution fusion | flops 1090535424 | bytes 71311360 | tf_op jit(solution)/shard_map/while/body/eval_jaxpr/dot_general | solution.py:41
  143.1 4.6 convolution_convert_fusion.3
  150.6 2.6 copy.21
  153.1 24.6 %convolution_add_fusion.2 = f32[256,32768]{1,0:T(8,128)} fusion(bf16[64,32768]{1,0:T(8,128)(2,1)S(1)} %bitcast.34, f32[256,32768]{1,0:T(8,128)} %get-tuple-element.281, pred[]{:T(512)S(6)} %compare.3, pred[256,32]{0,1:T(32,128)(4,1)S(1)} %fusion.34), kind=kOutput, calls=%fused_computation.3.clone.1 | convolution fusion | flops 1090535424 | bytes 71311360 | tf_op jit(solution)/shard_map/while/body/eval_jaxpr/dot_general | solution.py:41
  178.6 4.6 convolution_convert_fusion.3
  183.8 1.9 subtract_convert_fusion.2
  186.1 2.6 copy.21
  188.6 24.6 %convolution_add_fusion.2 = f32[256,32768]{1,0:T(8,128)} fusion(bf16[64,32768]{1,0:T(8,128)(2,1)S(1)} %bitcast.34, f32[256,32768]{1,0:T(8,128)} %get-tuple-element.281, pred[]{:T(512)S(6)} %compare.3, pred[256,32]{0,1:T(32,128)(4,1)S(1)} %fusion.34), kind=kOutput, calls=%fused_computation.3.clone.1 | convolution fusion | flops 1090535424 | bytes 71311360 | tf_op jit(solution)/shard_map/while/body/eval_jaxpr/dot_general | solution.py:41
  214.1 4.6 convolution_convert_fusion.3
  221.6 2.6 copy.21
  224.1 24.6 %convolution_add_fusion.2 = f32[256,32768]{1,0:T(8,128)} fusion(bf16[64,32768]{1,0:T(8,128)(2,1)S(1)} %bitcast.34, f32[256,32768]{1,0:T(8,128)} %get-tuple-element.281, pred[]{:T(512)S(6)} %compare.3, pred[256,32]{0,1:T(32,128)(4,1)S(1)} %fusion.34), kind=kOutput, calls=%fused_computation.3.clone.1 | convolution fusion | flops 1090535424 | bytes 71311360 | tf_op jit(solution)/shard_map/while/body/eval_jaxpr/dot_general | solution.py:41
  249.6 4.6 convolution_convert_fusion.3
  254.8 1.9 subtract_convert_fusion.2
  257.1 2.6 copy.21
  259.6 24.6 %convolution_add_fusion.2 = f32[256,32768]{1,0:T(8,128)} fusion(bf16[64,32768]{1,0:T(8,128)(2,1)S(1)} %bitcast.34, f32[256,32768]{1,0:T(8,128)} %get-tuple-element.281, pred[]{:T(512)S(6)} %compare.3, pred[256,32]{0,1:T(32,128)(4,1)S(1)} %fusion.34), kind=kOutput, calls=%fused_computation.3.clone.1 | convolution fusion | flops 1090535424 | bytes 71311360 | tf_op jit(solution)/shard_map/while/body/eval_jaxpr/dot_general | solution.py:41
  285.1 4.6 convolution_convert_fusion.3
  290.3 1.9 subtract_convert_fusion.2
  292.6 2.6 copy.21
  295.1 24.6 %convolution_add_fusion.2 = f32[256,32768]{1,0:T(8,128)} fusion(bf16[64,32768]{1,0:T(8,128)(2,1)S(1)} %bitcast.34, f32[256,32768]{1,0:T(8,128)} %get-tuple-element.281, pred[]{:T(512)S(6)} %compare.3, pred[256,32]{0,1:T(32,128)(4,1)S(1)} %fusion.34), kind=kOutput, calls=%fused_computation.3.clone.1 | convolution fusion | flops 1090535424 | bytes 71311360 | tf_op jit(solution)/shard_map/while/body/eval_jaxpr/dot_general | solution.py:41
  320.6 4.6 convolution_convert_fusion.3
  328.1 2.6 copy.21
  330.6 24.6 %convolution_add_fusion.2 = f32[256,32768]{1,0:T(8,128)} fusion(bf16[64,32768]{1,0:T(8,128)(2,1)S(1)} %bitcast.34, f32[256,32768]{1,0:T(8,128)} %get-tuple-element.281, pred[]{:T(512)S(6)} %compare.3, pred[256,32]{0,1:T(32,128)(4,1)S(1)} %fusion.34), kind=kOutput, calls=%fused_computation.3.clone.1 | convolution fusion | flops 1090535424 | bytes 71311360 | tf_op jit(solution)/shard_map/while/body/eval_jaxpr/dot_general | solution.py:41
  356.1 4.6 convolution_convert_fusion.3
  363.6 2.6 copy.21
  366.1 24.6 %convolution_add_fusion.2 = f32[256,32768]{1,0:T(8,128)} fusion(bf16[64,32768]{1,0:T(8,128)(2,1)S(1)} %bitcast.34, f32[256,32768]{1,0:T(8,128)} %get-tuple-element.281, pred[]{:T(512)S(6)} %compare.3, pred[256,32]{0,1:T(32,128)(4,1)S(1)} %fusion.34), kind=kOutput, calls=%fused_computation.3.clone.1 | convolution fusion | flops 1090535424 | bytes 71311360 | tf_op jit(solution)/shard_map/while/body/eval_jaxpr/dot_general | solution.py:41
  391.6 4.6 convolution_convert_fusion.3
  396.8 1.9 subtract_convert_fusion.2
  399.1 2.6 copy.21
  401.6 24.6 %convolution_add_fusion.2 = f32[256,32768]{1,0:T(8,128)} fusion(bf16[64,32768]{1,0:T(8,128)(2,1)S(1)} %bitcast.34, f32[256,32768]{1,0:T(8,128)} %get-tuple-element.281, pred[]{:T(512)S(6)} %compare.3, pred[256,32]{0,1:T(32,128)(4,1)S(1)} %fusion.34), kind=kOutput, calls=%fused_computation.3.clone.1 | convolution fusion | flops 1090535424 | bytes 71311360 | tf_op jit(solution)/shard_map/while/body/eval_jaxpr/dot_general | solution.py:41
  427.1 4.6 convolution_convert_fusion.3
  434.6 2.6 copy.21
  437.1 24.6 %convolution_add_fusion.2 = f32[256,32768]{1,0:T(8,128)} fusion(bf16[64,32768]{1,0:T(8,128)(2,1)S(1)} %bitcast.34, f32[256,32768]{1,0:T(8,128)} %get-tuple-element.281, pred[]{:T(512)S(6)} %compare.3, pred[256,32]{0,1:T(32,128)(4,1)S(1)} %fusion.34), kind=kOutput, calls=%fused_computation.3.clone.1 | convolution fusion | flops 1090535424 | bytes 71311360 | tf_op jit(solution)/shard_map/while/body/eval_jaxpr/dot_general | solution.py:41
  461.7 17.1 %convert_element_type.45 = bf16[256,32768]{1,0:T(8,128)(2,1)} convert(f32[256,32768]{1,0:T(8,128)} %get-tuple-element.171) | non-fusion elementwise | flops 8388608 | bytes 50331648 | tf_op jit(solution)/shard_map/convert_element_type | solution.py:47
  478.8 25.6 %convert_element_type.46 = bf16[32768,256]{1,0:T(8,128)(2,1)} reshape(bf16[256,32768]{1,0:T(8,128)(2,1)} %convert_element_type.45) | data formatting | bytes 33554432 | tf_op jit(solution)/shard_map/convert_element_type | solution.py:47
  504.7 145.2 %reduce-scatter.2.cloned.1.call-done = bf16[2048,256]{1,0:T(8,128)(2,1)} async-done(((bf16[32768,256]{1,0:T(8,128)(2,1)}), bf16[2048,256]{1,0:T(8,128)(2,1)}) %reduce-scatter.2.cloned.1.call-update) | async-done | bytes 1048592 | tf_op jit(solution)/shard_map/reduce_scatter | solution.py:46
  649.9 2.4 convolution_bitcast_fusion
  652.3 2.7 convolution_convert_fusion.1
  655.0 344.7 %all-gather.6.cloned.1.call-done = f32[32768,256]{0,1:T(8,128)} async-done(((f32[256,256]{0,1:T(8,128)}), f32[32768,256]{0,1:T(8,128)}) %all-gather.6.cloned.1.call-update) | async-done | bytes 33554448 | tf_op jit(solution)/shard_map/all_gather | solution.py:55
  999.7 19.6 %copy.17 = f32[32,8,128,256]{3,2,1,0:T(8,128)S(1)} copy(f32[32,8,128,256]{3,1,2,0:T(8,128)} %bitcast.38) | data formatting | bytes 67108864
  1019.3 4.1 bitcast_reduce_fusion
  (79 shorter events, 29.7 us)
Async XLA Ops:
  7.2 642.7 %copy-start = (bf16[2048,256]{1,0:T(8,128)(2,1)S(1)}, bf16[2048,256]{1,0:T(8,128)(2,1)}, u32[]{:S(2)}) copy-start(bf16[2048,256]{1,0:T(8,128)(2,1)} %param.12) | copy-start | bytes 3145732
  7.2 98.2 %all-gather.4.cloned.1.call-start = ((), (), s32[]{:S(2)}) async-start(), calls=%async_computation.1 | async-start | bytes 9437184 | tf_op jit(solution)/shard_map/all_gather | solution.py:12
  10.0 639.9 %reduce-scatter.2.cloned.1.call-start = ((), (), s32[]{:S(2)}) async-start(), calls=%async_computation.2 | async-start | bytes 17825792 | tf_op jit(solution)/shard_map/reduce_scatter | solution.py:46
  504.5 147.8 %copy-start.1 = (bf16[256,256]{1,0:T(8,128)(2,1)S(1)}, bf16[256,256]{1,0:T(8,128)(2,1)}, u32[]{:S(2)}) copy-start(bf16[256,256]{1,0:T(8,128)(2,1)} %param.13) | copy-start | bytes 393220
  504.5 495.2 %all-gather.6.cloned.1.call-start = ((), (), s32[]{:S(2)}) async-start(), calls=%async_computation.3 | async-start | bytes 33816576 | tf_op jit(solution)/shard_map/all_gather | solution.py:55
Sparse Core Ops, SparseCore 0:
  10.2 95.1 all-gather.3
  504.6 145.2 reduce-scatter.1
  652.4 347.2 all-gather.5
